TPU v7x, 32 devices: a whole 2x2x4 slice. The times are simulated.
32 devices in a mesh: grp: 4 (over x, core), ctx: 4 (over z), wt: 2 (over y).
Axes of the slice: x: 2, y: 2, z: 4, core: 2. Of those that a mesh axis runs over, the one named last changes fastest.
Arguments:
- tokens: bfloat16 [8, 2048, 1280], P(('grp', 'wt'), 'ctx'), may hold values from -6 to 6
- segments: int32 [8, 2048], P(('grp', 'wt')), may hold values from 0 to 2, as said below
- w_qkv: bfloat16 [1280, 3840], P('wt'), may hold values from -0.15625 to 0.15625
- w_proj: bfloat16 [1280, 1280], P('wt'), may hold values from -1.25 to 1.25
- w_in: bfloat16 [1280, 1280], P('wt'), may hold values from -0.15625 to 0.15625
- w_out: bfloat16 [1280, 1280], P('wt'), may hold values from -0.15625 to 0.15625
- gain_attn: float32 [1280], replicated, may hold values from 0.5 to 1.5
- gain_mlp: float32 [1280], replicated, may hold values from 0.5 to 1.5
- query_scale: float32 [80], replicated, may hold values from -0.5 to 1.5
- cotangent: bfloat16 [8, 2048, 1280], P(('grp', 'wt'), 'ctx'), may hold values from -6 to 6
Outputs:
- layer_out: bfloat16 [8, 2048, 1280], P(('grp', 'wt'), 'ctx')
- grad_tokens: bfloat16 [8, 2048, 1280], P(('grp', 'wt'), 'ctx')
- grad_w_qkv: float32 [1280, 3840], P('wt')
- grad_w_proj: float32 [1280, 1280], P('wt')
- grad_w_in: float32 [1280, 1280], P('wt')
- grad_w_out: float32 [1280, 1280], P('wt')
- grad_gain_attn: float32 [1280], replicated
- grad_gain_mlp: float32 [1280], replicated
- grad_query_scale: float32 [80], replicated
Inputs may be any that keep to these rules, and one draw needn't show every extreme that they name: `segments`: in each group the id starts at 0, never falls, and every id of 0 to 2 is used. Segment 0 ends 1024 - r tokens into the group, r below 256; each later continuation starts 512 + j tokens after the one before, j within 128 either way; the last runs to the group's end.
All inputs are finite; a program needn't handle non-finite values.
Results may differ from a plain program's by a relative error of at most 0.02.
Values may be sent and summed in bfloat16 or wider, within the bound.
No kernel may reach another device: no remote copies, remote signals or barrier semaphores. Data moves between devices by JAX's collectives and lax.ppermute only.
A program may use at most 256 MiB of HBM per device.

v0:
```python
import math
import jax
import jax.numpy as jnp
from jax import lax
from jax.sharding import PartitionSpec as P

D = 1280
H = 16
HD = 80
epsilon = 1e-06
scale_base = 1.442695041
masked_fill = -1e30


def rms_inverse(values):
    return lax.rsqrt(jnp.mean(values * values, axis=-1, keepdims=True) + epsilon)


def norm_back(values, inverse, grad_scaled):
    return inverse * grad_scaled - values * (inverse * inverse * inverse) * jnp.mean(
        grad_scaled * values, axis=-1, keepdims=True
    )


def times_trans(left, right):
    return lax.dot_general(
        left, right, (((1,), (1,)), ((), ())), preferred_element_type=jnp.float32
    )


def trans_times(left, right):
    return lax.dot_general(
        left, right, (((0,), (0,)), ((), ())), preferred_element_type=jnp.float32
    )


def visible(query_pos, query_seg, seg_row, offset, key_count):
    key_pos = offset + jnp.arange(key_count, dtype=jnp.int32)
    key_seg = lax.dynamic_slice_in_dim(seg_row, offset, key_count)
    return (key_pos[None, :] <= query_pos[:, None]) & (
        (key_seg[None, :] == 0) | (key_seg[None, :] == query_seg[:, None])
    )


def blocked(step_fn, carried, shard_rows):
    length = shard_rows.shape[0]
    width = math.gcd(length, 512)

    def advance(counter, carried_in):
        beginning = counter * width
        subrows = lax.dynamic_slice_in_dim(shard_rows, beginning, width, 0)
        return step_fn(carried_in, subrows, beginning)

    return lax.fori_loop(0, length // width, advance, carried)


def local(
    tokens, segments, w_qkv, w_proj, w_in, w_out, gain_attn, gain_mlp, query_scale, cotangent
):
    inputs = tokens[0].astype(jnp.float32)
    rows = inputs.shape[0]
    seg_row = segments[0]
    group_len = seg_row.shape[0]
    own_index = lax.axis_index("ctx")
    own_offset = own_index * rows
    query_pos = own_offset + jnp.arange(rows, dtype=jnp.int32)
    query_seg = lax.dynamic_slice_in_dim(seg_row, own_offset, rows)
    full_qkv, full_proj, full_in, full_out = (
        lax.all_gather(w_qkv, "wt", axis=0, tiled=True),
        lax.all_gather(w_proj, "wt", axis=0, tiled=True),
        lax.all_gather(w_in, "wt", axis=0, tiled=True),
        lax.all_gather(w_out, "wt", axis=0, tiled=True),
    )
    inverse_attn = rms_inverse(inputs)
    normed = (inputs * inverse_attn * gain_attn).astype(jnp.bfloat16)
    project = jnp.dot(normed, full_qkv, preferred_element_type=jnp.float32)
    dim_scale = scale_base / math.sqrt(HD) * jax.nn.softplus(query_scale)
    raw_queries = project[:, :D].reshape(rows, H, HD)
    queries = (raw_queries * dim_scale).astype(jnp.bfloat16)
    keyval = project[:, D:].astype(jnp.bfloat16)

    def forward_step(carried, subrows, offset):
        running_max, running_sum, accum = carried
        key_count = subrows.shape[0]
        keys_part = subrows[:, :D].reshape(key_count, H, HD)
        values_part = subrows[:, D:].reshape(key_count, H, HD)
        scores = jnp.einsum("qhd,khd->hqk", queries, keys_part, preferred_element_type=jnp.float32)
        allowed = visible(query_pos, query_seg, seg_row, offset, key_count)[None]
        masked = jnp.where(allowed, scores, masked_fill)
        new_max = jnp.maximum(running_max, jnp.max(masked, axis=-1))
        factor = jnp.exp(running_max - new_max)
        exponent = jnp.where(allowed, jnp.exp(masked - new_max[:, :, None]), 0.0)
        running_sum = running_sum * factor + jnp.sum(exponent, axis=-1)
        accum = accum * jnp.transpose(factor)[:, :, None] + jnp.einsum(
            "hqk,khd->qhd",
            exponent.astype(jnp.bfloat16),
            values_part,
            preferred_element_type=jnp.float32,
        )
        return (new_max, running_sum, accum)

    start_state = (
        jnp.full((H, rows), masked_fill, jnp.float32),
        jnp.zeros((H, rows), jnp.float32),
        jnp.zeros((rows, H, HD), jnp.float32),
    )
    running_max, running_sum, accum = blocked(
        forward_step, start_state, lax.all_gather(keyval, "ctx", axis=0, tiled=True)
    )
    logsum = running_max + jnp.log(running_sum)
    attn_float = accum / jnp.transpose(running_sum)[:, :, None]
    attended = attn_float.reshape(rows, D).astype(jnp.bfloat16)
    resid = inputs + jnp.dot(attended, full_proj, preferred_element_type=jnp.float32)
    inverse_mlp = rms_inverse(resid)
    normed_mlp = (resid * inverse_mlp * gain_mlp).astype(jnp.bfloat16)
    hidden = jnp.dot(normed_mlp, full_in, preferred_element_type=jnp.float32)
    active = jax.nn.silu(hidden).astype(jnp.bfloat16)
    layer_out = (resid + jnp.dot(active, full_out, preferred_element_type=jnp.float32)).astype(
        jnp.bfloat16
    )
    back_qkv, back_proj, back_in, back_out = (
        lax.all_gather(w_qkv, "wt", axis=0, tiled=True),
        lax.all_gather(w_proj, "wt", axis=0, tiled=True),
        lax.all_gather(w_in, "wt", axis=0, tiled=True),
        lax.all_gather(w_out, "wt", axis=0, tiled=True),
    )
    grad_out = cotangent[0].astype(jnp.float32)
    grad_mlp = cotangent[0]
    grad_active = times_trans(grad_mlp, back_out)
    grad_w_out = trans_times(active, grad_mlp)
    sigmoid_h = jax.nn.sigmoid(hidden)
    grad_hidden = (grad_active * sigmoid_h * (1.0 + hidden * (1.0 - sigmoid_h))).astype(
        jnp.bfloat16
    )
    grad_w_in = trans_times(normed_mlp, grad_hidden)
    grad_normed_mlp = times_trans(grad_hidden, back_in)
    grad_gain_mlp = jnp.sum(grad_normed_mlp * resid * inverse_mlp, axis=0)
    grad_resid = grad_out + norm_back(resid, inverse_mlp, grad_normed_mlp * gain_mlp)
    grad_proj = grad_resid.astype(jnp.bfloat16)
    grad_w_proj = trans_times(attended, grad_proj)
    grad_attended = times_trans(grad_proj, back_proj).astype(jnp.bfloat16).reshape(rows, H, HD)
    delta = jnp.transpose(jnp.sum(grad_attended.astype(jnp.float32) * attn_float, axis=-1))

    def backward_step(carried, subrows, offset):
        grad_queries, grad_keyval = carried
        key_count = subrows.shape[0]
        keys_part = subrows[:, :D].reshape(key_count, H, HD)
        values_part = subrows[:, D:].reshape(key_count, H, HD)
        scores = jnp.einsum("qhd,khd->hqk", queries, keys_part, preferred_element_type=jnp.float32)
        allowed = visible(query_pos, query_seg, seg_row, offset, key_count)[None]
        probs = jnp.where(
            allowed, jnp.exp(jnp.where(allowed, scores, masked_fill) - logsum[:, :, None]), 0.0
        )
        grad_probs = jnp.einsum(
            "qhd,khd->hqk", grad_attended, values_part, preferred_element_type=jnp.float32
        )
        grad_scores = (probs * (grad_probs - delta[:, :, None])).astype(jnp.bfloat16)
        grad_queries = grad_queries + jnp.einsum(
            "hqk,khd->qhd", grad_scores, keys_part, preferred_element_type=jnp.float32
        )
        grad_keys = jnp.einsum(
            "hqk,qhd->khd", grad_scores, queries, preferred_element_type=jnp.float32
        )
        grad_values = jnp.einsum(
            "hqk,qhd->khd",
            probs.astype(jnp.bfloat16),
            grad_attended,
            preferred_element_type=jnp.float32,
        )
        combined = jnp.concatenate(
            [grad_keys.reshape(key_count, D), grad_values.reshape(key_count, D)], axis=1
        )
        current = lax.dynamic_slice_in_dim(grad_keyval, offset, key_count, 0)
        grad_keyval = lax.dynamic_update_slice_in_dim(grad_keyval, current + combined, offset, 0)
        return (grad_queries, grad_keyval)

    back_state = (jnp.zeros((rows, H, HD), jnp.float32), jnp.zeros((group_len, 2 * D), jnp.float32))
    grad_queries, grad_keyval = blocked(
        backward_step, back_state, lax.all_gather(keyval, "ctx", axis=0, tiled=True)
    )
    grad_keyval_own = lax.psum_scatter(
        grad_keyval.astype(jnp.bfloat16), "ctx", scatter_dimension=0, tiled=True
    ).astype(jnp.float32)
    grad_dims = jnp.sum(grad_queries * raw_queries, axis=(0, 1))
    grad_query_scale = grad_dims * (scale_base / math.sqrt(HD)) * jax.nn.sigmoid(query_scale)
    grad_project = jnp.concatenate(
        [(grad_queries * dim_scale).reshape(rows, D), grad_keyval_own], axis=1
    ).astype(jnp.bfloat16)
    grad_w_qkv = trans_times(normed, grad_project)
    grad_normed = times_trans(grad_project, back_qkv)
    grad_gain_attn = jnp.sum(grad_normed * inputs * inverse_attn, axis=0)
    grad_tokens = (grad_resid + norm_back(inputs, inverse_attn, grad_normed * gain_attn)).astype(
        jnp.bfloat16
    )
    shard_qkv, shard_proj, shard_in, shard_out = (
        lax.psum_scatter(
            grad_w_qkv.astype(jnp.bfloat16), "wt", scatter_dimension=0, tiled=True
        ).astype(jnp.float32),
        lax.psum_scatter(
            grad_w_proj.astype(jnp.bfloat16), "wt", scatter_dimension=0, tiled=True
        ).astype(jnp.float32),
        lax.psum_scatter(
            grad_w_in.astype(jnp.bfloat16), "wt", scatter_dimension=0, tiled=True
        ).astype(jnp.float32),
        lax.psum_scatter(
            grad_w_out.astype(jnp.bfloat16), "wt", scatter_dimension=0, tiled=True
        ).astype(jnp.float32),
    )
    total_qkv, total_proj, total_in, total_out = (
        lax.psum(shard_qkv.astype(jnp.bfloat16), ("grp", "ctx")).astype(jnp.float32),
        lax.psum(shard_proj.astype(jnp.bfloat16), ("grp", "ctx")).astype(jnp.float32),
        lax.psum(shard_in.astype(jnp.bfloat16), ("grp", "ctx")).astype(jnp.float32),
        lax.psum(shard_out.astype(jnp.bfloat16), ("grp", "ctx")).astype(jnp.float32),
    )
    total_gain_attn, total_gain_mlp, total_scale = lax.psum(
        (grad_gain_attn, grad_gain_mlp, grad_query_scale), ("grp", "ctx", "wt")
    )
    return (
        layer_out[None],
        grad_tokens[None],
        total_qkv,
        total_proj,
        total_in,
        total_out,
        total_gain_attn,
        total_gain_mlp,
        total_scale,
    )


def solution(mesh):
    placed = (
        P(("grp", "wt"), "ctx", None),
        P(("grp", "wt"), None),
        P("wt", None),
        P("wt", None),
        P("wt", None),
        P("wt", None),
        P(),
        P(),
        P(),
        P(("grp", "wt"), "ctx", None),
    )
    return jax.shard_map(
        local,
        mesh=mesh,
        in_specs=placed,
        out_specs=(
            P(("grp", "wt"), "ctx", None),
            P(("grp", "wt"), "ctx", None),
            P("wt", None),
            P("wt", None),
            P("wt", None),
            P("wt", None),
            P(),
            P(),
            P(),
        ),
        check_vma=False,
    )
```

profile of v0, /device:TPU:0, one launch (start us, length us, event | category | flops | bytes accessed | tf_op | source)
XLA Modules:
  0.0 1364.7 jit_solution(8203904737533730321)
XLA Ops:
  9.4 125.2 %all-gather.6.cloned.1.call-done = bf16[1280,3840]{1,0:T(8,128)(2,1)} async-done(((bf16[640,3840]{1,0:T(8,128)(2,1)}), bf16[1280,3840]{1,0:T(8,128)(2,1)}) %all-gather.6.cloned.1.call-update) | async-done | bytes 9830416 | tf_op jit(solution)/shard_map/all_gather | solution.py:69
  156.0 175.5 %all-gather.8.cloned.1.call-done = bf16[2048,2560]{1,0:T(8,128)(2,1)} async-done(((bf16[512,2560]{1,0:T(8,128)(2,1)}), bf16[2048,2560]{1,0:T(8,128)(2,1)}) %all-gather.8.cloned.1.call-update) | async-done | bytes 10485776 | tf_op jit(solution)/shard_map/all_gather | solution.py:108
  331.5 14.6 %copy.34 = bf16[2048,2560]{0,1:T(8,128)(2,1)} copy(bf16[2048,2560]{1,0:T(8,128)(2,1)} %all-gather.8.cloned.1.call-done) | data formatting | bytes 20971520
  346.1 122.1 %while.34 = (s32[]{:T(128)}, f32[16,512]{1,0:T(8,128)S(1)}, f32[16,512]{1,0:T(8,128)S(1)}, f32[512,16,80]{0,2,1:T(8,128)}, s32[2048]{0:T(1024)S(1)}, /*index=5*/...) while((s32[]{:T(128)}, f32[16,512]{1,0:T(8,128)S(1)}, ...), condition=%wide.region_4.5_spmd.clone, body=%wide.region_1.4_spmd.clone.sunk | while | flops 1387185664 | bytes 66340068 | solution.py:54
  386.8 10.0 fusion.115
  396.7 10.4 bitcast_add_fusion.4
  427.0 10.7 bitcast_add_fusion.4
  457.5 10.4 bitcast_add_fusion.4
  510.4 188.2 %while.35 = (s32[]{:T(128)}, f32[512,16,80]{0,2,1:T(8,128)}, f32[2048,2560]{0,1:T(8,128)}, bf16[2048,2560]{0,1:T(8,128)(2,1)}, s32[2048]{0:T(1024)S(1)}, /*index...) while((s32[]{:T(128)}, f32[512,16,80]{0,2,1:T(8,128)}, ...), condition=%wide.region_9.10_spmd.clone, body=%wide.region_8.9_spmd.clone.sunk | while | flops 3402368512 | bytes 138003792 | solution.py:54
  523.4 11.4 fusion.130
  534.8 9.7 fusion.129
  569.0 11.4 fusion.130
  616.4 11.4 fusion.130
  663.7 11.4 fusion.130
  698.6 12.3 convert_element_type.118
  736.2 151.1 %reduce-scatter.6.cloned.1.call-done = bf16[512,2560]{0,1:T(8,128)(2,1)} async-done(((bf16[2048,2560]{0,1:T(8,128)(2,1)}), bf16[512,2560]{0,1:T(8,128)(2,1)}) %reduce-scatter.6.cloned.1.call-update) | async-done | bytes 2621456 | tf_op jit(solution)/shard_map/reduce_scatter | solution.py:181
  887.3 10.9 convolution_convert_fusion
  898.4 37.5 %reduce-scatter.12.cloned.1.call-done = bf16[640,1280]{1,0:T(8,128)(2,1)} async-done(((bf16[1280,1280]{1,0:T(8,128)(2,1)}), bf16[640,1280]{1,0:T(8,128)(2,1)}) %reduce-scatter.12.cloned.1.call-update) | async-done | bytes 1638416 | tf_op jit(solution)/shard_map/reduce_scatter | solution.py:202
  936.0 47.7 %reduce-scatter.14.cloned.1.call-done = bf16[640,1280]{1,0:T(8,128)(2,1)} async-done(((bf16[1280,1280]{1,0:T(8,128)(2,1)}), bf16[640,1280]{1,0:T(8,128)(2,1)}) %reduce-scatter.14.cloned.1.call-update) | async-done | bytes 1638416 | tf_op jit(solution)/shard_map/reduce_scatter | solution.py:205
  983.7 47.6 %reduce-scatter.10.cloned.1.call-done = bf16[640,1280]{1,0:T(8,128)(2,1)} async-done(((bf16[1280,1280]{1,0:T(8,128)(2,1)}), bf16[640,1280]{1,0:T(8,128)(2,1)}) %reduce-scatter.10.cloned.1.call-update) | async-done | bytes 1638416 | tf_op jit(solution)/shard_map/reduce_scatter | solution.py:199
  1031.3 117.7 %reduce-scatter.8.cloned.1.call-done = bf16[640,3840]{1,0:T(8,128)(2,1)} async-done(((bf16[1280,3840]{1,0:T(8,128)(2,1)}), bf16[640,3840]{1,0:T(8,128)(2,1)}) %reduce-scatter.8.cloned.1.call-update) | async-done | bytes 4915216 | tf_op jit(solution)/shard_map/reduce_scatter | solution.py:196
  1156.6 12.2 fusion.40
  1168.8 41.6 %all-reduce = (f32[1280]{0:T(1024)}, f32[1280]{0:T(1024)}, f32[80]{0:T(128)}) all-reduce(f32[1280]{0:T(1024)S(1)} %get-tuple-element.469, f32[1280]{0:T(1024)S(1)} %copy-done.24, f32[80]{0:T(128)S(1)} %divide_multiply_fusion), channel_id=1, replica_groups=mesh['grp'=4,'ctx'=4,'wt'=2] {'grp','ctx','wt'}, use_global_device_ids=true, to_apply=%region_21.22 | all-reduce | flops 2640 | bytes 21120 | tf_op jit(solution)/shard_map/psum | solution.py:215
  1214.8 131.1 %all-reduce.4.cloned.1.call-done = (bf16[640,3840]{1,0:T(8,128)(2,1)}, bf16[640,1280]{1,0:T(8,128)(2,1)}, bf16[640,1280]{1,0:T(8,128)(2,1)}, bf16[640,1280]{1,0:T(8,128)(2,1)}) async-done(((bf16[640,3840]{1,0:T(8,128)(2,1)}, bf16[640,1280]{1,0:T(8,128)(2,1)}, bf16[640,1280]{1,0:T(8,128)(2,1)}, bf16[640,1280]{1,0:T(8,128)(2,1)}), (bf16[640,3840]{1,0:T(8,128)(2,1)}, bf16[640,1280]{1,0:T(8,128)(2,1)}, ...) | async-done | bytes 9830416 | tf_op jit(solution)/shard_map/psum | solution.py:210
  (230 shorter events, 327.3 us)
Async XLA Ops:
  7.2 127.5 %copy-start.19 = (f32[1280]{0:T(1024)S(1)}, f32[1280]{0:T(1024)}, u32[]{:S(2)}) copy-start(f32[1280]{0:T(1024)} %param.20) | copy-start | bytes 15364
  7.2 127.4 %all-gather.6.cloned.1.call-start = ((), (), s32[]{:S(2)}) async-start(), calls=%async_computation.5 | async-start | bytes 14745600 | tf_op jit(solution)/shard_map/all_gather | solution.py:69
  7.9 323.5 %all-gather.8.cloned.1.call-start = ((), (), s32[]{:S(2)}) async-start(), calls=%async_computation.6 | async-start | bytes 13107200 | tf_op jit(solution)/shard_map/all_gather | solution.py:108
  9.4 132.9 %copy-start.22 = (f32[512]{0:T(512)}, f32[512]{0:T(512)S(1)}, u32[]{:S(2)}) copy-start(f32[512]{0:T(512)S(1)} %get-tuple-element.537) | copy-start | bytes 6148
  147.4 324.1 %all-gather.10.cloned.1.call-start = ((), (), s32[]{:S(2)}) async-start(), calls=%async_computation.7 | async-start | bytes 4915200 | tf_op jit(solution)/shard_map/all_gather | solution.py:70
  148.1 329.2 %all-gather.12.cloned.1.call-start = ((), (), s32[]{:S(2)}) async-start(), calls=%async_computation.8 | async-start | bytes 4915200 | tf_op jit(solution)/shard_map/all_gather | solution.py:71
  148.7 334.9 %all-gather.14.cloned.1.call-start = ((), (), s32[]{:S(2)}) async-start(), calls=%async_computation.9 | async-start | bytes 4915200 | tf_op jit(solution)/shard_map/all_gather | solution.py:72
  149.3 738.0 %reduce-scatter.6.cloned.1.call-start = ((), (), s32[]{:S(2)}) async-start(), calls=%async_computation.10 | async-start | bytes 13107200 | tf_op jit(solution)/shard_map/reduce_scatter | solution.py:181
  477.3 14.2 %copy-start.27 = (f32[512]{0:T(512)}, f32[512]{0:T(512)S(1)}, u32[]{:S(2)}) copy-start(f32[512]{0:T(512)S(1)} %get-tuple-element.539) | copy-start | bytes 6148
  477.3 6.3 copy-start.16
  597.5 6.3 copy-start.12
  710.9 225.1 %reduce-scatter.12.cloned.1.call-start = ((), (), s32[]{:S(2)}) async-start(), calls=%async_computation.13 | async-start | bytes 4915200 | tf_op jit(solution)/shard_map/reduce_scatter | solution.py:202
  717.6 266.1 %reduce-scatter.14.cloned.1.call-start = ((), (), s32[]{:S(2)}) async-start(), calls=%async_computation.14 | async-start | bytes 4915200 | tf_op jit(solution)/shard_map/reduce_scatter | solution.py:205
  724.4 307.0 %reduce-scatter.10.cloned.1.call-start = ((), (), s32[]{:S(2)}) async-start(), calls=%async_computation.12 | async-start | bytes 4915200 | tf_op jit(solution)/shard_map/reduce_scatter | solution.py:199
  731.0 418.0 %reduce-scatter.8.cloned.1.call-start = ((), (), s32[]{:S(2)}) async-start(), calls=%async_computation.11 | async-start | bytes 14745600 | tf_op jit(solution)/shard_map/reduce_scatter | solution.py:196
  732.7 154.6 %copy-start.20 = (f32[1280]{0:T(1024)S(1)}, f32[1280]{0:T(1024)}, u32[]{:S(2)}) copy-start(f32[1280]{0:T(1024)} %param.20) | copy-start | bytes 15364
  732.7 154.6 %copy-start.23 = (f32[512]{0:T(512)S(1)}, f32[512]{0:T(512)}, u32[]{:S(2)}) copy-start(f32[512]{0:T(512)} %copy-done.22) | copy-start | bytes 6148
  898.2 447.7 %all-reduce.4.cloned.1.call-start = ((), (), s32[]{:S(2)}) async-start(), calls=%async_computation.15 | async-start | bytes 19660800 | tf_op jit(solution)/shard_map/psum | solution.py:210
  1149.7 6.9 copy-start.4
  1149.7 6.9 copy-start.15
  1149.7 6.9 copy-start.32
  1156.6 12.2 copy-start.24
  1156.6 53.8 %copy-start.21 = (f32[512]{0:T(512)S(1)}, f32[512]{0:T(512)}, u32[]{:S(2)}) copy-start(f32[512]{0:T(512)} %get-tuple-element.536) | copy-start | bytes 6148
  1345.9 7.5 slice-start.1
  (35 other events, 95.9 us)
Sparse Core Ops, SparseCore 0:
  9.6 125.0 all-gather.5
  147.5 183.9 all-gather.7
  333.0 44.5 all-gather.9
  379.0 46.4 all-gather.11
  426.9 46.3 all-gather.13
  711.0 176.2 reduce-scatter.5
  890.1 45.8 reduce-scatter.11
  938.9 44.7 reduce-scatter.13
  986.5 44.7 reduce-scatter.9
  1034.2 114.7 reduce-scatter.7
  1153.0 192.8 all-reduce.3
where the time goes:
time: 1370 us; the launch traced here: 1360 us
  waiting for transfers between devices  836 us (61%)
  matrix products  296 us (22%)
  other arithmetic  108 us (8%)
  local copies, waits for them, and re-layouts  67.2 us (5%)
  blocking collectives  41.6 us (3%)
  between operations  14.5 us (1%)
    all_gather x1, waiting for transfers between devices, local(): lax.all_gather(keyval, 'ctx', axis=0, tiled=True)  175 us
    reduce_scatter x1, waiting for transfers between devices, local(): lax.psum_scatter(grad_keyval.astype(jnp.bfloat16), 'ctx', scatter_dimensi...  151 us
    psum x1, waiting for transfers between devices, local(): lax.psum(shard_qkv.astype(jnp.bfloat16), ('grp', 'ctx')).astype(jnp.float32)  131 us
    all_gather x1, waiting for transfers between devices, local(): lax.all_gather(w_qkv, 'wt', axis=0, tiled=True)  125 us
    reduce_scatter x1, waiting for transfers between devices, local(): lax.psum_scatter(grad_w_qkv.astype(jnp.bfloat16), 'wt', scatter_dimension...  118 us
    reduce_scatter x1, waiting for transfers between devices, local(): lax.psum_scatter(grad_w_out.astype(jnp.bfloat16), 'wt', scatter_dimension...  47.7 us
    reduce_scatter x1, waiting for transfers between devices, local(): lax.psum_scatter(grad_w_proj.astype(jnp.bfloat16), 'wt', scatter_dimensio...  47.6 us
    dot_general x4, matrix products, backward_step(): jnp.einsum('hqk,qhd->khd', probs.astype(jnp.bfloat16), grad_attended, pre...  45.8 us
  transfers between devices with their start and end apart: 11, of which 8 were waited for; matrix products, arithmetic and copies ran while one was open for 15% of the time, Pallas kernels for 0%

commit v1 on v0

--- a/solution.py
+++ b/solution.py
@@ -3,6 +3,7 @@
 import jax.numpy as jnp
 from jax import lax
 from jax.sharding import PartitionSpec as P
+from jax.lax import psum
 
 D = 1280
 H = 16
@@ -212,8 +213,11 @@
         lax.psum(shard_in.astype(jnp.bfloat16), ("grp", "ctx")).astype(jnp.float32),
         lax.psum(shard_out.astype(jnp.bfloat16), ("grp", "ctx")).astype(jnp.float32),
     )
-    total_gain_attn, total_gain_mlp, total_scale = lax.psum(
-        (grad_gain_attn, grad_gain_mlp, grad_query_scale), ("grp", "ctx", "wt")
+    set_arrays_for = lambda u_in, mesh_ax, axis_id: psum(
+        psum(u_in, axis_name=mesh_ax), axis_name=axis_id
+    )
+    total_gain_attn, total_gain_mlp, total_scale = set_arrays_for(
+        (grad_gain_attn, grad_gain_mlp, grad_query_scale), ("ctx", "wt"), "grp"
     )
     return (
         layer_out[None],

time: 1370 us -> 1370 us (level)
    psum x1 -> x2, blocking collectives: 41.6 us -> 49.2 us  [the longest x1 37.6 us: local(): psum(u_in, axis_name=mesh_ax)]
where the time goes in v1:
time: 1370 us; the launch traced here: 1360 us
  waiting for transfers between devices  828 us (60%)
  matrix products  296 us (22%)
  other arithmetic  108 us (8%)
  local copies, waits for them, and re-layouts  67.2 us (5%)
  blocking collectives  49.2 us (4%)
  between operations  14.5 us (1%)
    all_gather x1, waiting for transfers between devices, local(): lax.all_gather(keyval, 'ctx', axis=0, tiled=True)  175 us
    reduce_scatter x1, waiting for transfers between devices, local(): lax.psum_scatter(grad_keyval.astype(jnp.bfloat16), 'ctx', scatter_dimensi...  151 us
    all_gather x1, waiting for transfers between devices, local(): lax.all_gather(w_qkv, 'wt', axis=0, tiled=True)  125 us
    psum x1, waiting for transfers between devices, local(): lax.psum(shard_qkv.astype(jnp.bfloat16), ('grp', 'ctx')).astype(jnp.float32)  123 us
    reduce_scatter x1, waiting for transfers between devices, local(): lax.psum_scatter(grad_w_qkv.astype(jnp.bfloat16), 'wt', scatter_dimension...  118 us
    reduce_scatter x1, waiting for transfers between devices, local(): lax.psum_scatter(grad_w_out.astype(jnp.bfloat16), 'wt', scatter_dimension...  47.7 us
    reduce_scatter x1, waiting for transfers between devices, local(): lax.psum_scatter(grad_w_proj.astype(jnp.bfloat16), 'wt', scatter_dimensio...  47.6 us
    dot_general x4, matrix products, backward_step(): jnp.einsum('hqk,qhd->khd', probs.astype(jnp.bfloat16), grad_attended, pre...  45.8 us
  transfers between devices with their start and end apart: 11, of which 8 were waited for; matrix products, arithmetic and copies ran while one was open for 15% of the time, Pallas kernels for 0%

profile of v1, /device:TPU:0, one launch (start us, length us, event | category | flops | bytes accessed | tf_op | source)
XLA Modules:
  0.0 1364.5 jit_solution(5558013914821766928)
XLA Ops:
  9.4 125.2 %all-gather.6.cloned.1.call-done = bf16[1280,3840]{1,0:T(8,128)(2,1)} async-done(((bf16[640,3840]{1,0:T(8,128)(2,1)}), bf16[1280,3840]{1,0:T(8,128)(2,1)}) %all-gather.6.cloned.1.call-update) | async-done | bytes 9830416 | tf_op jit(solution)/shard_map/all_gather | solution.py:70
  156.0 175.5 %all-gather.8.cloned.1.call-done = bf16[2048,2560]{1,0:T(8,128)(2,1)} async-done(((bf16[512,2560]{1,0:T(8,128)(2,1)}), bf16[2048,2560]{1,0:T(8,128)(2,1)}) %all-gather.8.cloned.1.call-update) | async-done | bytes 10485776 | tf_op jit(solution)/shard_map/all_gather | solution.py:109
  331.5 14.7 %copy.34 = bf16[2048,2560]{0,1:T(8,128)(2,1)} copy(bf16[2048,2560]{1,0:T(8,128)(2,1)} %all-gather.8.cloned.1.call-done) | data formatting | bytes 20971520
  346.1 122.2 %while.34 = (s32[]{:T(128)}, f32[16,512]{1,0:T(8,128)S(1)}, f32[16,512]{1,0:T(8,128)S(1)}, f32[512,16,80]{0,2,1:T(8,128)}, s32[2048]{0:T(1024)S(1)}, /*index=5*/...) while((s32[]{:T(128)}, f32[16,512]{1,0:T(8,128)S(1)}, ...), condition=%wide.region_4.5_spmd.clone, body=%wide.region_1.4_spmd.clone.sunk | while | flops 1387185664 | bytes 66340068 | solution.py:55
  386.9 9.9 fusion.115
  396.8 10.4 bitcast_add_fusion.4
  427.1 10.8 bitcast_add_fusion.4
  457.6 10.4 bitcast_add_fusion.4
  510.5 188.1 %while.35 = (s32[]{:T(128)}, f32[512,16,80]{0,2,1:T(8,128)}, f32[2048,2560]{0,1:T(8,128)}, bf16[2048,2560]{0,1:T(8,128)(2,1)}, s32[2048]{0:T(1024)S(1)}, /*index...) while((s32[]{:T(128)}, f32[512,16,80]{0,2,1:T(8,128)}, ...), condition=%wide.region_9.10_spmd.clone, body=%wide.region_8.9_spmd.clone.sunk | while | flops 3402368512 | bytes 138003792 | solution.py:55
  523.5 11.4 fusion.130
  569.1 11.4 fusion.130
  616.4 11.4 fusion.130
  663.7 11.4 fusion.130
  698.6 12.3 convert_element_type.118
  736.3 151.1 %reduce-scatter.6.cloned.1.call-done = bf16[512,2560]{0,1:T(8,128)(2,1)} async-done(((bf16[2048,2560]{0,1:T(8,128)(2,1)}), bf16[512,2560]{0,1:T(8,128)(2,1)}) %reduce-scatter.6.cloned.1.call-update) | async-done | bytes 2621456 | tf_op jit(solution)/shard_map/reduce_scatter | solution.py:182
  887.4 10.9 convolution_convert_fusion
  898.5 37.5 %reduce-scatter.12.cloned.1.call-done = bf16[640,1280]{1,0:T(8,128)(2,1)} async-done(((bf16[1280,1280]{1,0:T(8,128)(2,1)}), bf16[640,1280]{1,0:T(8,128)(2,1)}) %reduce-scatter.12.cloned.1.call-update) | async-done | bytes 1638416 | tf_op jit(solution)/shard_map/reduce_scatter | solution.py:203
  936.0 47.7 %reduce-scatter.14.cloned.1.call-done = bf16[640,1280]{1,0:T(8,128)(2,1)} async-done(((bf16[1280,1280]{1,0:T(8,128)(2,1)}), bf16[640,1280]{1,0:T(8,128)(2,1)}) %reduce-scatter.14.cloned.1.call-update) | async-done | bytes 1638416 | tf_op jit(solution)/shard_map/reduce_scatter | solution.py:206
  983.8 47.6 %reduce-scatter.10.cloned.1.call-done = bf16[640,1280]{1,0:T(8,128)(2,1)} async-done(((bf16[1280,1280]{1,0:T(8,128)(2,1)}), bf16[640,1280]{1,0:T(8,128)(2,1)}) %reduce-scatter.10.cloned.1.call-update) | async-done | bytes 1638416 | tf_op jit(solution)/shard_map/reduce_scatter | solution.py:200
  1031.4 117.7 %reduce-scatter.8.cloned.1.call-done = bf16[640,3840]{1,0:T(8,128)(2,1)} async-done(((bf16[1280,3840]{1,0:T(8,128)(2,1)}), bf16[640,3840]{1,0:T(8,128)(2,1)}) %reduce-scatter.8.cloned.1.call-update) | async-done | bytes 4915216 | tf_op jit(solution)/shard_map/reduce_scatter | solution.py:197
  1156.7 12.2 fusion.40
  1168.9 37.6 %all-reduce = (f32[1280]{0:T(1024)S(1)}, f32[1280]{0:T(1024)S(1)}, f32[80]{0:T(128)S(1)}) all-reduce(f32[1280]{0:T(1024)S(1)} %get-tuple-element.469, f32[1280]{0:T(1024)S(1)} %copy-done.24, f32[80]{0:T(128)S(1)} %divide_multiply_fusion), channel_id=1, replica_groups=mesh['grp'=4,'ctx'=4,'wt'=2] {'ctx','wt'}, use_global_device_ids=true, to_apply=%region_21.22 | all-reduce | flops 2640 | bytes 21120 | tf_op jit(solution)/shard_map/psum | solution.py:217
  1206.4 11.6 all-reduce.1
  1222.4 123.2 %all-reduce.5.cloned.1.call-done = (bf16[640,3840]{1,0:T(8,128)(2,1)}, bf16[640,1280]{1,0:T(8,128)(2,1)}, bf16[640,1280]{1,0:T(8,128)(2,1)}, bf16[640,1280]{1,0:T(8,128)(2,1)}) async-done(((bf16[640,3840]{1,0:T(8,128)(2,1)}, bf16[640,1280]{1,0:T(8,128)(2,1)}, bf16[640,1280]{1,0:T(8,128)(2,1)}, bf16[640,1280]{1,0:T(8,128)(2,1)}), (bf16[640,3840]{1,0:T(8,128)(2,1)}, bf16[640,1280]{1,0:T(8,128)(2,1)}, ...) | async-done | bytes 9830416 | tf_op jit(solution)/shard_map/psum | solution.py:211
  (231 shorter events, 336.9 us)
Async XLA Ops:
  7.2 127.5 %copy-start.19 = (f32[1280]{0:T(1024)S(1)}, f32[1280]{0:T(1024)}, u32[]{:S(2)}) copy-start(f32[1280]{0:T(1024)} %param.20) | copy-start | bytes 15364
  7.2 127.4 %all-gather.6.cloned.1.call-start = ((), (), s32[]{:S(2)}) async-start(), calls=%async_computation.5 | async-start | bytes 14745600 | tf_op jit(solution)/shard_map/all_gather | solution.py:70
  7.9 323.5 %all-gather.8.cloned.1.call-start = ((), (), s32[]{:S(2)}) async-start(), calls=%async_computation.6 | async-start | bytes 13107200 | tf_op jit(solution)/shard_map/all_gather | solution.py:109
  9.4 132.9 %copy-start.22 = (f32[512]{0:T(512)}, f32[512]{0:T(512)S(1)}, u32[]{:S(2)}) copy-start(f32[512]{0:T(512)S(1)} %get-tuple-element.540) | copy-start | bytes 6148
  147.4 324.2 %all-gather.10.cloned.1.call-start = ((), (), s32[]{:S(2)}) async-start(), calls=%async_computation.7 | async-start | bytes 4915200 | tf_op jit(solution)/shard_map/all_gather | solution.py:71
  148.1 329.3 %all-gather.12.cloned.1.call-start = ((), (), s32[]{:S(2)}) async-start(), calls=%async_computation.8 | async-start | bytes 4915200 | tf_op jit(solution)/shard_map/all_gather | solution.py:72
  148.7 335.0 %all-gather.14.cloned.1.call-start = ((), (), s32[]{:S(2)}) async-start(), calls=%async_computation.9 | async-start | bytes 4915200 | tf_op jit(solution)/shard_map/all_gather | solution.py:73
  149.3 738.1 %reduce-scatter.6.cloned.1.call-start = ((), (), s32[]{:S(2)}) async-start(), calls=%async_computation.10 | async-start | bytes 13107200 | tf_op jit(solution)/shard_map/reduce_scatter | solution.py:182
  477.4 14.2 %copy-start.27 = (f32[512]{0:T(512)}, f32[512]{0:T(512)S(1)}, u32[]{:S(2)}) copy-start(f32[512]{0:T(512)S(1)} %get-tuple-element.542) | copy-start | bytes 6148
  477.5 6.3 copy-start.16
  692.2 6.3 copy-start.12
  710.9 225.1 %reduce-scatter.12.cloned.1.call-start = ((), (), s32[]{:S(2)}) async-start(), calls=%async_computation.13 | async-start | bytes 4915200 | tf_op jit(solution)/shard_map/reduce_scatter | solution.py:203
  717.7 266.1 %reduce-scatter.14.cloned.1.call-start = ((), (), s32[]{:S(2)}) async-start(), calls=%async_computation.14 | async-start | bytes 4915200 | tf_op jit(solution)/shard_map/reduce_scatter | solution.py:206
  724.4 307.0 %reduce-scatter.10.cloned.1.call-start = ((), (), s32[]{:S(2)}) async-start(), calls=%async_computation.12 | async-start | bytes 4915200 | tf_op jit(solution)/shard_map/reduce_scatter | solution.py:200
  731.1 418.0 %reduce-scatter.8.cloned.1.call-start = ((), (), s32[]{:S(2)}) async-start(), calls=%async_computation.11 | async-start | bytes 14745600 | tf_op jit(solution)/shard_map/reduce_scatter | solution.py:197
  732.8 154.6 %copy-start.20 = (f32[1280]{0:T(1024)S(1)}, f32[1280]{0:T(1024)}, u32[]{:S(2)}) copy-start(f32[1280]{0:T(1024)} %param.20) | copy-start | bytes 15364
  732.8 154.6 %copy-start.23 = (f32[512]{0:T(512)S(1)}, f32[512]{0:T(512)}, u32[]{:S(2)}) copy-start(f32[512]{0:T(512)} %copy-done.22) | copy-start | bytes 6148
  898.3 447.4 %all-reduce.5.cloned.1.call-start = ((), (), s32[]{:S(2)}) async-start(), calls=%async_computation.15 | async-start | bytes 19660800 | tf_op jit(solution)/shard_map/psum | solution.py:211
  1149.8 6.9 copy-start.4
  1149.8 6.9 copy-start.15
  1149.8 6.9 copy-start.32
  1156.7 12.2 copy-start.24
  1156.7 61.4 %copy-start.21 = (f32[512]{0:T(512)S(1)}, f32[512]{0:T(512)}, u32[]{:S(2)}) copy-start(f32[512]{0:T(512)} %get-tuple-element.539) | copy-start | bytes 6148
  1345.6 7.5 slice-start.1
  (35 other events, 95.9 us)
Sparse Core Ops, SparseCore 0:
  9.6 125.0 all-gather.5
  147.5 183.9 all-gather.7
  333.0 44.5 all-gather.9
  379.0 46.4 all-gather.11
  426.9 46.4 all-gather.13
  711.1 176.2 reduce-scatter.5
  890.2 45.8 reduce-scatter.11
  939.0 44.7 reduce-scatter.13
  986.6 44.7 reduce-scatter.9
  1034.3 114.7 reduce-scatter.7
  1153.1 192.5 all-reduce.4
